TPU v7x, 512 devices: a whole 4x8x8 slice. The times are simulated.
512 devices in a mesh: occ: 64 (over x, y, core), aux: 8 (over z).
Axes of the slice: x: 4, y: 8, z: 8, core: 2. Of those that a mesh axis runs over, the one named last changes fastest.
Arguments:
- ao_blocks: bfloat16 [256, 256, 8192], P('occ', None, 'aux'), may hold values from -0.59765625 to 0.59765625
- pno_coef: bfloat16 [1024, 256, 200], P('occ'), may hold values from -0.375 to 0.375
- pno_energy: float32 [1024, 200], P('occ'), may hold values from 0.3 to 3
- occ_energy: float32 [256], replicated, may hold values from -1.5 to -0.3
- pair_partner: int32 [1024], P('occ'), may hold values from 0 to 255, as said below
- pno_count: int32 [1024], P('occ'), may hold values from 40 to 200, as said below
Outputs:
- amplitudes: float32 [1024, 200, 200], P(('occ', 'aux'))
- orbital_pair_energy: float32 [256], P('occ')
Inputs may be any that keep to these rules, and one draw needn't show every extreme that they name: pair_partner[s] differs from own(s) and is an orbital owned by the same index of occ as own(s), or by the index just below or just above it. `pno_count`: every count is a multiple of 8; in every block of 16 pairs one count is 200 and one is 40.
All inputs are finite; a program needn't handle non-finite values.
Results may differ from a plain program's by a relative error of at most 0.0041.
Values may be sent and summed in bfloat16 or wider, within the bound.
A program may use at most 128 MiB of HBM per device.

v0:
```python
import jax
import jax.numpy as jnp
from jax import lax
from jax.sharding import PartitionSpec as P


def padded(cells, sides, width):
    for axis, dim in sides:
        count = lax.axis_size(axis)
        ends = count - 1
        head = lax.slice_in_dim(cells, 0, width, axis=dim)
        tail = lax.slice_in_dim(cells, cells.shape[dim] - width, cells.shape[dim], axis=dim)
        cells = jnp.concatenate(
            [
                lax.ppermute(tail, axis, [(i, (i + 1) % count) for i in range(ends)]),
                cells,
                lax.ppermute(head, axis, [((i + 1) % count, i) for i in range(ends)]),
            ],
            axis=dim,
        )
    return cells


def shards(ao_blocks, pno_coef, pno_energy, occ_energy, pair_partner, pno_count):
    orb_dev = ao_blocks.shape[0]
    virtuals = ao_blocks.shape[1]
    aux_block = ao_blocks.shape[2]
    pair_dev = pno_coef.shape[0]
    pno_max = pno_coef.shape[2]
    per_orbital = pair_dev // orb_dev
    occ_place = lax.axis_index("occ")
    aux_place = lax.axis_index("aux")
    columns = jnp.arange(pno_max, dtype=jnp.int32)
    kept_mask = (columns[None, :] < pno_count[:, None]).astype(jnp.bfloat16)
    masked_coef = pno_coef * kept_mask[:, None, :]
    projected_own = (
        jnp.einsum(
            "ornp,onk->orpk",
            masked_coef.reshape(orb_dev, per_orbital, virtuals, pno_max),
            ao_blocks,
            preferred_element_type=jnp.float32,
        )
        .astype(jnp.bfloat16)
        .reshape(pair_dev, pno_max, aux_block)
    )
    nearby = padded(ao_blocks, (("occ", 0),), orb_dev)
    window_slot = pair_partner - (occ_place - 1) * orb_dev
    partner_blocks = jnp.take(nearby, window_slot, axis=0)
    projected_partner = jnp.einsum(
        "snp,snk->spk", masked_coef, partner_blocks, preferred_element_type=jnp.float32
    ).astype(jnp.bfloat16)
    partials = jnp.einsum(
        "spk,sqk->spq", projected_own, projected_partner, preferred_element_type=jnp.float32
    )
    share_rows = pair_dev // lax.axis_size("aux")
    first_row = aux_place * share_rows
    totals = lax.psum(partials, "aux")
    exchange_ints = lax.dynamic_slice_in_dim(totals, first_row, share_rows, 0)
    own_orbital = occ_place * orb_dev + jnp.arange(pair_dev, dtype=jnp.int32) // per_orbital
    mine_owner = lax.dynamic_slice_in_dim(own_orbital, first_row, share_rows, 0)
    mine_partner = lax.dynamic_slice_in_dim(pair_partner, first_row, share_rows, 0)
    energies = lax.dynamic_slice_in_dim(pno_energy, first_row, share_rows, 0)
    shift_occ = occ_energy[mine_owner] + occ_energy[mine_partner]
    denominator = energies[:, :, None] + energies[:, None, :] - shift_occ[:, None, None]
    amplitudes = -exchange_ints / denominator
    pair_energy = jnp.sum(
        (2.0 * exchange_ints - jnp.swapaxes(exchange_ints, 1, 2)) * amplitudes, axis=(1, 2)
    )
    half_energy = 0.5 * pair_energy
    orbital_ids = jnp.arange(occ_energy.shape[0], dtype=jnp.int32)
    hits = (orbital_ids[None, :] == mine_owner[:, None]).astype(jnp.float32) + (
        orbital_ids[None, :] == mine_partner[:, None]
    ).astype(jnp.float32)
    spread = jnp.sum(hits * half_energy[:, None], axis=0)
    whole_sum = lax.psum(spread, ("occ", "aux"))
    orbital = lax.dynamic_slice_in_dim(whole_sum, occ_place * orb_dev, orb_dev, 0)
    return (amplitudes, orbital)


def solution(mesh):
    return jax.shard_map(
        shards,
        mesh=mesh,
        in_specs=(
            P("occ", None, "aux"),
            P("occ", None, None),
            P("occ", None),
            P(),
            P("occ"),
            P("occ"),
        ),
        out_specs=(P(("occ", "aux"), None, None), P("occ")),
        check_vma=False,
    )
```

profile of v0, /device:TPU:1, one launch (start us, length us, event | category | flops | bytes accessed | tf_op | source)
XLA Modules:
  0.0 275.3 jit_solution(15171100014383080903)
XLA Ops:
  7.2 0.0 copy-start
  7.2 0.0 copy-start.2
  7.2 0.0 all-reduce.2.cloned.1.call-start
  7.2 4.7 %collective-permute-start = (bf16[4,256,1024]{2,1,0:T(8,128)(2,1)}, bf16[4,256,1024]{2,1,0:T(8,128)(2,1)}, u32[]{:S(2)}, u32[]{:S(2)}) collective-permute-start(bf16[4,256,1024]{2,1,0:T(8,128)(2,1)} %param.6), channel_id=1, source_target_pairs={{0,8},{8,16},{16,24},{24,32},{32,40},{40,48},{48,56},{56,64},{64,7... | collective-permute-start | bytes 6291464 | tf_op jit(solution)/shard_map/ppermute | solution.py:15
  12.0 6.8 %collective-permute-start.1 = (bf16[4,256,1024]{2,1,0:T(8,128)(2,1)}, bf16[4,256,1024]{2,1,0:T(8,128)(2,1)}, u32[]{:S(2)}, u32[]{:S(2)}) collective-permute-start(bf16[4,256,1024]{2,1,0:T(8,128)(2,1)} %param.6), channel_id=1, source_target_pairs={{8,0},{16,8},{24,16},{32,24},{40,32},{48,40},{56,48},{64,56},{72,6... | collective-permute-start | bytes 6291464 | tf_op jit(solution)/shard_map/ppermute | solution.py:17
  18.7 0.7 compare_and_fusion
  19.4 0.7 fusion.13
  20.1 1.9 broadcast_multiply_fusion
  22.0 0.0 copy-start.3
  22.1 0.0 copy-done.2
  22.1 4.7 %convolution_convert_fusion = bf16[4,4,200,1024]{3,2,1,0:T(8,128)(2,1)} fusion(bf16[4,4,256,200]{2,3,1,0:T(8,128)(2,1)S(1)} %bitcast.16, bf16[4,256,1024]{2,1,0:T(8,128)(2,1)S(1)} %copy-done.2), kind=kOutput, calls=%fused_computation.8 | convolution fusion | flops 1680998400 | bytes 10289152 | tf_op jit(solution)/shard_map/ornp,onk->orpk/dot_general | solution.py:37
  26.8 0.0 copy-done.3
  26.8 8.5 %collective-permute-done = bf16[4,256,1024]{2,1,0:T(8,128)(2,1)} collective-permute-done((bf16[4,256,1024]{2,1,0:T(8,128)(2,1)}, bf16[4,256,1024]{2,1,0:T(8,128)(2,1)}, u32[]{:S(2)}, u32[]{:S(2)}) %collective-permute-start) | collective-permute-done | bytes 2097184 | tf_op jit(solution)/shard_map/ppermute | solution.py:15
  35.2 4.4 %collective-permute-done.1 = bf16[4,256,1024]{2,1,0:T(8,128)(2,1)} collective-permute-done((bf16[4,256,1024]{2,1,0:T(8,128)(2,1)}, bf16[4,256,1024]{2,1,0:T(8,128)(2,1)}, u32[]{:S(2)}, u32[]{:S(2)}) %collective-permute-start.1) | collective-permute-done | bytes 2097184 | tf_op jit(solution)/shard_map/ppermute | solution.py:17
  39.6 5.5 %pad_maximum_fusion = bf16[12,256,1024]{2,1,0:T(8,128)(2,1)} fusion(bf16[4,256,1024]{2,1,0:T(8,128)(2,1)} %collective-permute-done.1, bf16[4,256,1024]{2,1,0:T(8,128)(2,1)S(1)} %copy-done.2, bf16[4,256,1024]{2,1,0:T(8,128)(2,1)} %collective-permute-done), kind=kLoop, calls=%fused_computation.7 | loop fusion | flops 6291456 | bytes 12582912 | tf_op jit(solution)/shard_map/concatenate | solution.py:13
  45.1 0.0 copy-start.4
  45.1 7.7 %gather_fusion = bf16[16,256,1024]{2,1,0:T(8,128)(2,1)} fusion(bf16[12,256,1024]{2,1,0:T(8,128)(2,1)} %pad_maximum_fusion, s32[1024]{0:T(1024)S(1)} %pad_clamp_fusion.2), kind=kCustom, calls=%fused_computation | custom fusion | bytes 16777280 | tf_op jit(solution)/shard_map/jit(_take)/gather | solution.py:48
  52.8 0.0 copy-done.4
  52.8 0.0 copy-start.5
  52.8 0.0 copy-start.1
  52.8 10.8 %fusion.9 = f32[16,200,200]{2,1,0:T(8,128)} fusion(bf16[16,200,1024]{2,1,0:T(8,128)(2,1)} %bitcast.17, bf16[16,256,200]{1,2,0:T(8,128)(2,1)S(1)} %copy-done.4, bf16[16,256,1024]{2,1,0:T(8,128)(2,1)} %gather_fusion, pred[16]{0:T(512)(128)(4,1)S(1)} %get-tuple-element.12), kind=kOutput, calls=%fused_computation.11 | convolution fusion | flops 2995912704 | bytes 19140624 | tf_op jit(solution)/shard_map/spk,sqk->spq/dot_general | solution.py:52
  63.6 0.0 all-reduce.2.cloned.1.call-update
  63.6 0.0 copy-done.5
  63.6 0.1 compare_select_fusion
  63.7 0.0 copy-done.1
  63.7 0.6 gather_fusion.1
  64.3 0.6 gather_fusion.2
  65.0 0.0 copy-done
  65.0 102.3 %all-reduce.2.cloned.1.call-done = f32[16,200,200]{2,1,0:T(8,128)} async-done(((f32[16,200,200]{2,1,0:T(8,128)}), f32[16,200,200]{2,1,0:T(8,128)}) %all-reduce.2.cloned.1.call-update) | async-done | bytes 2560016 | tf_op jit(solution)/shard_map/psum | solution.py:57
  167.3 1.0 constant_dynamic-slice_fusion.1
  168.3 0.2 copy.14
  168.5 1.3 fusion.12
  169.8 0.9 copy.16
  170.8 0.1 fusion.16
  170.8 97.1 %psum.15 = f32[256]{0:T(256)S(1)} all-reduce(f32[256]{0:T(256)S(1)} %fusion.16), channel_id=1, replica_groups=mesh['occ'=64,'aux'=8] {'occ','aux'}, use_global_device_ids=true, to_apply=%region_3.4 | all-reduce | flops 256 | bytes 2048 | tf_op jit(solution)/shard_map/psum | solution.py:75
  267.9 0.6 dynamic_slice.19
  (7 shorter events, 0.0 us)
Async XLA Ops:
  7.2 57.8 %copy-start = (f32[16,200]{1,0:T(8,128)S(1)}, f32[16,200]{1,0:T(8,128)}, u32[]{:S(2)}) copy-start(f32[16,200]{1,0:T(8,128)} %param.8) | copy-start | bytes 38404
  7.2 14.9 %copy-start.2 = (bf16[4,256,1024]{2,1,0:T(8,128)(2,1)S(1)}, bf16[4,256,1024]{2,1,0:T(8,128)(2,1)}, u32[]{:S(2)}) copy-start(bf16[4,256,1024]{2,1,0:T(8,128)(2,1)} %param.6) | copy-start | bytes 6291460
  7.2 160.1 %all-reduce.2.cloned.1.call-start = ((), (), s32[]{:S(2)}) async-start(), calls=%async_computation | async-start | bytes 6553600 | tf_op jit(solution)/shard_map/psum | solution.py:57
  7.2 28.0 %collective-permute-start = (bf16[4,256,1024]{2,1,0:T(8,128)(2,1)}, bf16[4,256,1024]{2,1,0:T(8,128)(2,1)}, u32[]{:S(2)}, u32[]{:S(2)}) collective-permute-start(bf16[4,256,1024]{2,1,0:T(8,128)(2,1)} %param.6), channel_id=1, source_target_pairs={{0,8},{8,16},{16,24},{24,32},{32,40},{40,48},{48,56},{56,64},{64,7... | collective-permute-start | bytes 6291464 | tf_op jit(solution)/shard_map/ppermute | solution.py:15
  12.0 27.7 %collective-permute-start.1 = (bf16[4,256,1024]{2,1,0:T(8,128)(2,1)}, bf16[4,256,1024]{2,1,0:T(8,128)(2,1)}, u32[]{:S(2)}, u32[]{:S(2)}) collective-permute-start(bf16[4,256,1024]{2,1,0:T(8,128)(2,1)} %param.6), channel_id=1, source_target_pairs={{8,0},{16,8},{24,16},{32,24},{40,32},{48,40},{56,48},{64,56},{72,6... | collective-permute-start | bytes 6291464 | tf_op jit(solution)/shard_map/ppermute | solution.py:17
  22.0 4.7 %copy-start.3 = (bf16[16,256,200]{1,2,0:T(8,128)(2,1)}, bf16[16,256,200]{1,2,0:T(8,128)(2,1)S(1)}, u32[]{:S(2)}) copy-start(bf16[16,256,200]{1,2,0:T(8,128)(2,1)S(1)} %broadcast_multiply_fusion) | copy-start | bytes 4915204
  45.1 7.7 %copy-start.4 = (bf16[16,256,200]{1,2,0:T(8,128)(2,1)S(1)}, bf16[16,256,200]{1,2,0:T(8,128)(2,1)}, u32[]{:S(2)}) copy-start(bf16[16,256,200]{1,2,0:T(8,128)(2,1)} %copy-done.3) | copy-start | bytes 4915204
  52.8 10.8 %copy-start.5 = (s32[16]{0:T(128)S(1)}, s32[16]{0:T(128)}, u32[]{:S(2)}) copy-start(s32[16]{0:T(128)} %param.10) | copy-start | bytes 196
  52.8 10.9 %copy-start.1 = (f32[256]{0:T(256)S(1)}, f32[256]{0:T(256)}, u32[]{:S(2)}) copy-start(f32[256]{0:T(256)} %param.9) | copy-start | bytes 3076
Sparse Core Ops, SparseCore 0:
  63.7 103.5 all-reduce.1
where the time goes:
time: 276 us; the launch traced here: 275 us
  waiting for transfers between devices  115 us (42%)
  blocking collectives  97.1 us (35%)
  matrix products  15.4 us (6%)
  between operations  14.1 us (5%)
  local copies, waits for them, and re-layouts  11.7 us (4%)
  starting transfers between devices  11.5 us (4%)
  other arithmetic  10.3 us (4%)
    psum x1, waiting for transfers between devices, shards(): totals = lax.psum(partials, 'aux')  102 us
    psum x1, blocking collectives, shards(): whole_sum = lax.psum(spread, ('occ', 'aux'))  97.1 us
    dot_general x1, matrix products, shards(): jnp.einsum('spk,sqk->spq', projected_own, projected_partner, preferred_el...  10.8 us
    ppermute x1, waiting for transfers between devices, padded(): lax.ppermute(tail, axis, [(i, (i + 1) % count) for i in range(ends)])  8.47 us
    gather x1, local copies, waits for them, and re-layouts, shards(): partner_blocks = jnp.take(nearby, window_slot, axis=0)  7.67 us
    ppermute x1, starting transfers between devices, padded(): lax.ppermute(head, axis, [((i + 1) % count, i) for i in range(ends)])  6.75 us
  transfers between devices with their start and end apart: 3, of which 3 were waited for; matrix products, arithmetic and copies ran while one was open for 3% of the time, Pallas kernels for 0%

commit v1 on v0

--- a/solution.py
+++ b/solution.py
@@ -54,7 +54,11 @@
     )
     share_rows = pair_dev // lax.axis_size("aux")
     first_row = aux_place * share_rows
-    totals = lax.psum(partials, "aux")
+    peers = lax.axis_size("aux")
+    totals, hop = (partials, 1)
+    while hop < peers:
+        totals = totals + lax.ppermute(totals, "aux", [(i_2, i_2 ^ hop) for i_2 in range(peers)])
+        hop = 2 * hop
     exchange_ints = lax.dynamic_slice_in_dim(totals, first_row, share_rows, 0)
     own_orbital = occ_place * orb_dev + jnp.arange(pair_dev, dtype=jnp.int32) // per_orbital
     mine_owner = lax.dynamic_slice_in_dim(own_orbital, first_row, share_rows, 0)

time: 276 us -> 572 us (2.07)
  waiting for transfers between devices: 115 us -> 414 us
  between operations: 14.1 us -> 0.79 us
  starting transfers between devices: 11.5 us -> 21.4 us
    ppermute x0 -> x3, waiting for transfers between devices: none -> 401 us  [shards(): lax.ppermute(totals, 'aux', [(i_2, i_2 ^ hop) for i_2 in range(peers)])]
    psum x1 -> x0, waiting for transfers between devices: 102 us -> none  [shards(): totals = lax.psum(partials, 'aux')]
    ppermute x0 -> x3, starting transfers between devices: none -> 9.95 us  [shards(): lax.ppermute(totals, 'aux', [(i_2, i_2 ^ hop) for i_2 in range(peers)])]
  transfers between devices with their start and end apart: 3 -> 5, of which waited for: 3 -> 5; matrix products, arithmetic and copies ran while one was open for 3% -> 2% of each run, Pallas kernels for 0% -> 0%
where the time goes in v1:
time: 572 us; the launch traced here: 571 us
  waiting for transfers between devices  414 us (72%)
  blocking collectives  93.2 us (16%)
  starting transfers between devices  21.4 us (4%)
  matrix products  15.4 us (3%)
  other arithmetic  14.9 us (3%)
  local copies, waits for them, and re-layouts  11.7 us (2%)
    ppermute x3, waiting for transfers between devices, shards(): lax.ppermute(totals, 'aux', [(i_2, i_2 ^ hop) for i_2 in range(peers)])  401 us
    psum x1, blocking collectives, shards(): whole_sum = lax.psum(spread, ('occ', 'aux'))  93.2 us
  transfers between devices with their start and end apart: 5, of which 5 were waited for; matrix products, arithmetic and copies ran while one was open for 2% of the time, Pallas kernels for 0%

profile of v1, /device:TPU:1, one launch (start us, length us, event | category | flops | bytes accessed | tf_op | source)
XLA Modules:
  0.0 571.2 jit_solution(9641644705544006679)
XLA Ops:
  0.6 0.0 copy-start
  0.6 0.0 copy-start.2
  0.7 4.7 collective-permute-start
  5.4 6.7 %collective-permute-start.1 = (bf16[4,256,1024]{2,1,0:T(8,128)(2,1)}, bf16[4,256,1024]{2,1,0:T(8,128)(2,1)}, u32[]{:S(2)}, u32[]{:S(2)}) collective-permute-start(bf16[4,256,1024]{2,1,0:T(8,128)(2,1)} %param.6), channel_id=1, source_target_pairs={{8,0},{16,8},{24,16},{32,24},{40,32},{48,40},{56,48},{64,56},{72,6... | collective-permute-start | bytes 6291464 | tf_op jit(solution)/shard_map/ppermute | solution.py:17
  12.1 0.7 compare_and_fusion
  12.8 0.7 fusion.13
  13.5 1.9 broadcast_multiply_fusion
  15.5 0.0 copy-start.3
  15.5 0.0 copy-done.2
  15.5 4.7 convolution_convert_fusion
  20.2 0.0 copy-done.3
  20.2 8.5 %collective-permute-done = bf16[4,256,1024]{2,1,0:T(8,128)(2,1)} collective-permute-done((bf16[4,256,1024]{2,1,0:T(8,128)(2,1)}, bf16[4,256,1024]{2,1,0:T(8,128)(2,1)}, u32[]{:S(2)}, u32[]{:S(2)}) %collective-permute-start) | collective-permute-done | bytes 2097184 | tf_op jit(solution)/shard_map/ppermute | solution.py:15
  28.7 4.4 collective-permute-done.1
  33.0 5.5 pad_maximum_fusion
  38.5 0.0 copy-start.4
  38.5 7.7 %gather_fusion = bf16[16,256,1024]{2,1,0:T(8,128)(2,1)} fusion(bf16[12,256,1024]{2,1,0:T(8,128)(2,1)} %pad_maximum_fusion, s32[1024]{0:T(1024)S(1)} %pad_clamp_fusion.2), kind=kCustom, calls=%fused_computation | custom fusion | bytes 16777280 | tf_op jit(solution)/shard_map/jit(_take)/gather | solution.py:48
  46.2 0.0 copy-done.4
  46.2 10.7 %fusion.9 = f32[16,200,200]{2,1,0:T(8,128)} fusion(bf16[16,200,1024]{2,1,0:T(8,128)(2,1)} %bitcast.17, bf16[16,256,200]{1,2,0:T(8,128)(2,1)S(1)} %copy-done.4, bf16[16,256,1024]{2,1,0:T(8,128)(2,1)} %gather_fusion, pred[16]{0:T(512)(128)(4,1)S(1)} %get-tuple-element.12), kind=kOutput, calls=%fused_computation.11 | convolution fusion | flops 2995912704 | bytes 19140624 | tf_op jit(solution)/shard_map/spk,sqk->spq/dot_general | solution.py:52
  56.9 4.0 collective-permute-start.2
  60.9 62.6 %collective-permute-done.2 = f32[16,200,200]{2,1,0:T(8,128)S(1)} collective-permute-done((f32[16,200,200]{2,1,0:T(8,128)}, f32[16,200,200]{2,1,0:T(8,128)S(1)}, u32[]{:S(2)}, u32[]{:S(2)}) %collective-permute-start.2) | collective-permute-done | bytes 2560032 | tf_op jit(solution)/shard_map/ppermute | solution.py:60
  123.5 2.3 add.62
  125.8 0.0 copy-start.5
  125.8 0.0 copy-start.1
  125.8 4.0 collective-permute-start.3
  129.9 265.0 %collective-permute-done.3 = f32[16,200,200]{2,1,0:T(8,128)S(1)} collective-permute-done((f32[16,200,200]{2,1,0:T(8,128)S(1)}, f32[16,200,200]{2,1,0:T(8,128)S(1)}, u32[]{:S(2)}, u32[]{:S(2)}) %collective-permute-start.3) | collective-permute-done | bytes 2560032 | tf_op jit(solution)/shard_map/ppermute | solution.py:60
  394.9 0.4 add.63
  395.3 1.9 collective-permute-start.4
  397.2 0.0 copy-done.5
  397.3 0.1 compare_select_fusion
  397.4 0.0 copy-done.1
  397.4 0.6 gather_fusion.1
  398.0 0.6 gather_fusion.2
  398.6 0.0 copy-done
  398.7 73.4 %collective-permute-done.4 = f32[16,200,200]{2,1,0:T(8,128)} collective-permute-done((f32[16,200,200]{2,1,0:T(8,128)S(1)}, f32[16,200,200]{2,1,0:T(8,128)}, u32[]{:S(2)}, u32[]{:S(2)}) %collective-permute-start.4) | collective-permute-done | bytes 2560032 | tf_op jit(solution)/shard_map/ppermute | solution.py:60
  472.1 1.8 dynamic-slice_add_fusion
  473.9 1.2 copy.14
  475.1 1.3 fusion.12
  476.4 0.9 copy.16
  477.3 0.1 fusion.16
  477.4 93.2 %psum.7 = f32[256]{0:T(256)S(1)} all-reduce(f32[256]{0:T(256)S(1)} %fusion.16), channel_id=1, replica_groups=mesh['occ'=64,'aux'=8] {'occ','aux'}, use_global_device_ids=true, to_apply=%region_2.3 | all-reduce | flops 256 | bytes 2048 | tf_op jit(solution)/shard_map/psum | solution.py:79
  570.7 0.6 dynamic_slice.19
  (7 shorter events, 0.0 us)
Async XLA Ops:
  0.6 398.0 %copy-start = (f32[16,200]{1,0:T(8,128)S(1)}, f32[16,200]{1,0:T(8,128)}, u32[]{:S(2)}) copy-start(f32[16,200]{1,0:T(8,128)} %param.8) | copy-start | bytes 38404
  0.6 14.8 %copy-start.2 = (bf16[4,256,1024]{2,1,0:T(8,128)(2,1)S(1)}, bf16[4,256,1024]{2,1,0:T(8,128)(2,1)}, u32[]{:S(2)}) copy-start(bf16[4,256,1024]{2,1,0:T(8,128)(2,1)} %param.6) | copy-start | bytes 6291460
  0.7 28.0 %collective-permute-start = (bf16[4,256,1024]{2,1,0:T(8,128)(2,1)}, bf16[4,256,1024]{2,1,0:T(8,128)(2,1)}, u32[]{:S(2)}, u32[]{:S(2)}) collective-permute-start(bf16[4,256,1024]{2,1,0:T(8,128)(2,1)} %param.6), channel_id=1, source_target_pairs={{0,8},{8,16},{16,24},{24,32},{32,40},{40,48},{48,56},{56,64},{64,7... | collective-permute-start | bytes 6291464 | tf_op jit(solution)/shard_map/ppermute | solution.py:15
  5.4 27.7 %collective-permute-start.1 = (bf16[4,256,1024]{2,1,0:T(8,128)(2,1)}, bf16[4,256,1024]{2,1,0:T(8,128)(2,1)}, u32[]{:S(2)}, u32[]{:S(2)}) collective-permute-start(bf16[4,256,1024]{2,1,0:T(8,128)(2,1)} %param.6), channel_id=1, source_target_pairs={{8,0},{16,8},{24,16},{32,24},{40,32},{48,40},{56,48},{64,56},{72,6... | collective-permute-start | bytes 6291464 | tf_op jit(solution)/shard_map/ppermute | solution.py:17
  15.5 4.7 copy-start.3
  38.5 7.7 %copy-start.4 = (bf16[16,256,200]{1,2,0:T(8,128)(2,1)S(1)}, bf16[16,256,200]{1,2,0:T(8,128)(2,1)}, u32[]{:S(2)}) copy-start(bf16[16,256,200]{1,2,0:T(8,128)(2,1)} %copy-done.3) | copy-start | bytes 4915204
  56.9 66.6 %collective-permute-start.2 = (f32[16,200,200]{2,1,0:T(8,128)}, f32[16,200,200]{2,1,0:T(8,128)S(1)}, u32[]{:S(2)}, u32[]{:S(2)}) collective-permute-start(f32[16,200,200]{2,1,0:T(8,128)} %fusion.9), channel_id=1, source_target_pairs={{0,1},{1,0},{2,3},{3,2},{4,5},{5,4},{6,7},{7,6},{8,9},{9,8},{10,11... | collective-permute-start | bytes 7680008 | tf_op jit(solution)/shard_map/ppermute | solution.py:60
  125.8 271.4 %copy-start.5 = (s32[16]{0:T(128)S(1)}, s32[16]{0:T(128)}, u32[]{:S(2)}) copy-start(s32[16]{0:T(128)} %param.10) | copy-start | bytes 196
  125.8 271.5 %copy-start.1 = (f32[256]{0:T(256)S(1)}, f32[256]{0:T(256)}, u32[]{:S(2)}) copy-start(f32[256]{0:T(256)} %param.9) | copy-start | bytes 3076
  125.8 269.0 %collective-permute-start.3 = (f32[16,200,200]{2,1,0:T(8,128)S(1)}, f32[16,200,200]{2,1,0:T(8,128)S(1)}, u32[]{:S(2)}, u32[]{:S(2)}) collective-permute-start(f32[16,200,200]{2,1,0:T(8,128)S(1)} %add.62), channel_id=1, source_target_pairs={{0,2},{1,3},{2,0},{3,1},{4,6},{5,7},{6,4},{7,5},{8,10},{9,11},{10,... | collective-permute-start | bytes 7680008 | tf_op jit(solution)/shard_map/ppermute | solution.py:60
  395.3 76.8 %collective-permute-start.4 = (f32[16,200,200]{2,1,0:T(8,128)S(1)}, f32[16,200,200]{2,1,0:T(8,128)}, u32[]{:S(2)}, u32[]{:S(2)}) collective-permute-start(f32[16,200,200]{2,1,0:T(8,128)S(1)} %add.63), channel_id=1, source_target_pairs={{0,4},{1,5},{2,6},{3,7},{4,0},{5,1},{6,2},{7,3},{8,12},{9,13},{10,... | collective-permute-start | bytes 7680008 | tf_op jit(solution)/shard_map/ppermute | solution.py:60
